TPU v7x, 32 devices: a whole 2x2x4 slice. The times are simulated.
32 devices in a mesh: pix: 8 (over z, x), beam: 4 (over y, core).
Axes of the slice: x: 2, y: 2, z: 4, core: 2. Of those that a mesh axis runs over, the one named last changes fastest.
Arguments:
- sketch: bfloat16 [512, 128, 256], P('beam', 'pix'), may hold values from -6 to 6
- gains: bfloat16 [512, 32, 128, 128], P('pix', 'beam'), may hold values from -0.09375 to 0.09375
- coverage: int32 [512, 32], P('pix', 'beam'), may hold values from 0 to 127
Outputs:
- basis: float32 [512, 128, 256], P('beam', 'pix')
- factor: float32 [256, 256], replicated
Inputs may be any that keep to these rules, and one draw needn't show every extreme that they name: `coverage`: entries name beam blocks within the slot's group of 128 blocks; a block may be named by several slots.
All inputs are finite; a program needn't handle non-finite values.
Results may differ from a plain program's by a relative error of at most 0.0011.
Values may be sent and summed in bfloat16 or wider, within the bound.
No kernel may reach another device: no remote copies, remote signals or barrier semaphores. Data moves between devices by JAX's collectives and lax.ppermute only.
A program may use at most 192 MiB of HBM per device.

v0:
```python
import math
import jax
import jax.numpy as jnp
from jax import lax
from jax.sharding import PartitionSpec as P

BEAMS = 65536


def local(sketch, gains, coverage):
    tiles_here = gains.shape[0]
    slots_here = gains.shape[1]
    block_size = gains.shape[2]
    width = sketch.shape[2]
    blocks_here = sketch.shape[0]
    group_size = math.gcd(tiles_here, 8)
    group_count = tiles_here // group_size
    grouped_gains = gains.reshape(group_count, group_size, slots_here, block_size, block_size)
    grouped_ids = coverage.reshape(group_count, group_size, slots_here)
    full_sketch = lax.all_gather(sketch, "pix", axis=1, tiled=True)

    def pixel_pass(args):
        tile_gains, tile_ids = args
        picked = full_sketch[tile_ids]
        return jnp.einsum("tsab,tsbk->tak", tile_gains, picked, preferred_element_type=jnp.float32)

    partial_sketch = lax.map(pixel_pass, (grouped_gains, grouped_ids)).reshape(
        tiles_here, block_size, width
    )
    shares = lax.psum_scatter(partial_sketch, "beam", scatter_dimension=1, tiled=True).astype(
        jnp.bfloat16
    )
    rounded = lax.all_gather(shares, "beam", axis=1, tiled=True)
    grouped_rows = rounded.reshape(group_count, group_size, block_size, width)

    def step(total, args):
        tile_gains, tile_ids, tile_rows = args
        contrib = jnp.einsum(
            "tsab,tak->tsbk", tile_gains, tile_rows, preferred_element_type=jnp.float32
        )
        return (total.at[tile_ids.reshape(-1)].add(contrib.reshape(-1, block_size, width)), None)

    empty = jnp.zeros((blocks_here, block_size, width), jnp.float32)
    total, _ = lax.scan(step, empty, (grouped_gains, grouped_ids, grouped_rows))
    range_rows = lax.psum_scatter(total, "pix", scatter_dimension=1, tiled=True)
    flat = range_rows.reshape(-1, width)
    local_gram = jnp.dot(
        flat.T, flat, precision=lax.Precision.HIGHEST, preferred_element_type=jnp.float32
    )
    gram = lax.psum(local_gram, ("pix", "beam"))
    lower = jnp.linalg.cholesky(gram)
    solved = jax.scipy.linalg.solve_triangular(lower, flat.T, lower=True).T
    scale = jnp.sqrt(jnp.float32(BEAMS))
    return ((solved * scale).reshape(range_rows.shape), lower.T / scale)


def solution(mesh):
    return jax.shard_map(
        local,
        mesh=mesh,
        in_specs=(P("beam", "pix", None), P("pix", "beam", None, None), P("pix", "beam")),
        out_specs=(P("beam", "pix", None), P()),
        check_vma=False,
    )
```

profile of v0, /device:TPU:0, one launch (start us, length us, event | category | flops | bytes accessed | tf_op | source)
XLA Modules:
  0.0 1034.1 jit_solution(5837422681688760672)
XLA Ops:
  8.7 129.0 %all-gather.3.cloned.1.call-done = bf16[128,128,256]{2,1,0:T(8,128)(2,1)} async-done(((bf16[128,16,256]{2,1,0:T(8,128)(2,1)}), bf16[128,128,256]{2,1,0:T(8,128)(2,1)}) %all-gather.3.cloned.1.call-update) | async-done | bytes 8388624 | tf_op jit(solution)/shard_map/all_gather | solution.py:20
  137.7 86.9 %while.21 = (s32[]{:T(128)}, f32[8,8,128,256]{3,2,1,0:T(8,128)}, bf16[8,8,8,128,128]{4,3,2,1,0:T(8,128)(2,1)}, s32[8,8,8]{2,1,0:T(8,128)S(1)}, bf16[128,128,256]{2,1,0:T(8,128)(2,1)}, /*index=5*/s32[]{:T(128)}) while((s32[]{:T(128)}, f32[8,8,128,256]{3,2,1,0:T(8,128)}, bf16[8,8,8,128,128]{4,3,2,1,0:T(8,128)(2,1)}, s32[8,8,8]{2,1,0:T(8,128)S(1)}, ...), condition=%wide.region_1.2_spmd, body=%wide.region_0.1_spmd.sunk | while | flops 536872128 | bytes 15735369 | solution.py:27
  137.8 6.1 gather_fusion
  159.6 6.1 gather_fusion
  224.7 69.6 %reduce-scatter.3.cloned.1.call-done = f32[64,32,256]{2,1,0:T(8,128)} async-done(((f32[64,128,256]{2,1,0:T(8,128)}), f32[64,32,256]{2,1,0:T(8,128)}) %reduce-scatter.3.cloned.1.call-update) | async-done | bytes 2097168 | tf_op jit(solution)/shard_map/reduce_scatter | solution.py:30
  297.1 21.3 %copy.15 = bf16[64,8,128,128]{2,3,1,0:T(8,128)(2,1)} copy(bf16[64,8,128,128]{3,2,1,0:T(8,128)(2,1)} %bitcast.101) | data formatting | bytes 33554432 | tf_op args[1]
  318.3 13.3 %all-gather.5.cloned.1.call-done = bf16[64,128,256]{2,1,0:T(8,128)(2,1)} async-done(((bf16[64,32,256]{2,1,0:T(8,128)(2,1)}), bf16[64,128,256]{2,1,0:T(8,128)(2,1)}) %all-gather.5.cloned.1.call-update) | async-done | bytes 4194320 | tf_op jit(solution)/shard_map/all_gather | solution.py:33
  331.6 7.8 broadcast_in_dim.14
  339.4 206.6 %while.22 = (s32[]{:T(128)}, f32[128,128,256]{2,1,0:T(8,128)}, s32[8,8,8]{2,1,0:T(8,128)S(1)}, bf16[8,8,8,128,128]{3,4,2,1,0:T(8,128)(2,1)}, bf16[8,8,128,256]{3,2,1,0:T(8,128)(2,1)}, /*index=5*/s32[]{:T(128)}) while((s32[]{:T(128)}, f32[128,128,256]{2,1,0:T(8,128)}, s32[8,8,8]{2,1,0:T(8,128)S(1)}, bf16[8,8,8,128,128]{3,4,2,1,0:T(8,128)(2,1)}, ...), condition=%wide.region_5.6_spmd, body=%wide.region_3.5_spmd.sunk | while | flops 538968256 | bytes 36178760 | solution.py:44
  345.6 19.5 %scatter_fusion = f32[128,128,256]{2,1,0:T(8,128)} fusion(f32[128,128,256]{2,1,0:T(8,128)} %get-tuple-element.236, s32[64]{0:T(128)S(1)} %fusion.48, f32[64,128,256]{2,1,0:T(8,128)} %bitcast.97), kind=kCustom, calls=%fused_computation.1.clone.1 | custom fusion | flops 2097152 | bytes 25166080 | tf_op jit(solution)/shard_map/while/body/eval_jaxpr/scatter-add | solution.py:41
  371.3 19.7 %scatter_fusion = f32[128,128,256]{2,1,0:T(8,128)} fusion(f32[128,128,256]{2,1,0:T(8,128)} %get-tuple-element.236, s32[64]{0:T(128)S(1)} %fusion.48, f32[64,128,256]{2,1,0:T(8,128)} %bitcast.97), kind=kCustom, calls=%fused_computation.1.clone.1 | custom fusion | flops 2097152 | bytes 25166080 | tf_op jit(solution)/shard_map/while/body/eval_jaxpr/scatter-add | solution.py:41
  397.3 19.6 %scatter_fusion = f32[128,128,256]{2,1,0:T(8,128)} fusion(f32[128,128,256]{2,1,0:T(8,128)} %get-tuple-element.236, s32[64]{0:T(128)S(1)} %fusion.48, f32[64,128,256]{2,1,0:T(8,128)} %bitcast.97), kind=kCustom, calls=%fused_computation.1.clone.1 | custom fusion | flops 2097152 | bytes 25166080 | tf_op jit(solution)/shard_map/while/body/eval_jaxpr/scatter-add | solution.py:41
  423.1 19.6 %scatter_fusion = f32[128,128,256]{2,1,0:T(8,128)} fusion(f32[128,128,256]{2,1,0:T(8,128)} %get-tuple-element.236, s32[64]{0:T(128)S(1)} %fusion.48, f32[64,128,256]{2,1,0:T(8,128)} %bitcast.97), kind=kCustom, calls=%fused_computation.1.clone.1 | custom fusion | flops 2097152 | bytes 25166080 | tf_op jit(solution)/shard_map/while/body/eval_jaxpr/scatter-add | solution.py:41
  448.9 19.9 %scatter_fusion = f32[128,128,256]{2,1,0:T(8,128)} fusion(f32[128,128,256]{2,1,0:T(8,128)} %get-tuple-element.236, s32[64]{0:T(128)S(1)} %fusion.48, f32[64,128,256]{2,1,0:T(8,128)} %bitcast.97), kind=kCustom, calls=%fused_computation.1.clone.1 | custom fusion | flops 2097152 | bytes 25166080 | tf_op jit(solution)/shard_map/while/body/eval_jaxpr/scatter-add | solution.py:41
  475.0 19.3 %scatter_fusion = f32[128,128,256]{2,1,0:T(8,128)} fusion(f32[128,128,256]{2,1,0:T(8,128)} %get-tuple-element.236, s32[64]{0:T(128)S(1)} %fusion.48, f32[64,128,256]{2,1,0:T(8,128)} %bitcast.97), kind=kCustom, calls=%fused_computation.1.clone.1 | custom fusion | flops 2097152 | bytes 25166080 | tf_op jit(solution)/shard_map/while/body/eval_jaxpr/scatter-add | solution.py:41
  500.5 19.6 %scatter_fusion = f32[128,128,256]{2,1,0:T(8,128)} fusion(f32[128,128,256]{2,1,0:T(8,128)} %get-tuple-element.236, s32[64]{0:T(128)S(1)} %fusion.48, f32[64,128,256]{2,1,0:T(8,128)} %bitcast.97), kind=kCustom, calls=%fused_computation.1.clone.1 | custom fusion | flops 2097152 | bytes 25166080 | tf_op jit(solution)/shard_map/while/body/eval_jaxpr/scatter-add | solution.py:41
  526.3 19.6 %scatter_fusion = f32[128,128,256]{2,1,0:T(8,128)} fusion(f32[128,128,256]{2,1,0:T(8,128)} %get-tuple-element.236, s32[64]{0:T(128)S(1)} %fusion.48, f32[64,128,256]{2,1,0:T(8,128)} %bitcast.97), kind=kCustom, calls=%fused_computation.1.clone.1 | custom fusion | flops 2097152 | bytes 25166080 | tf_op jit(solution)/shard_map/while/body/eval_jaxpr/scatter-add | solution.py:41
  546.2 280.3 %reduce-scatter.5.cloned.1.call-done = f32[128,16,256]{2,1,0:T(8,128)} async-done(((f32[128,128,256]{2,1,0:T(8,128)}), f32[128,16,256]{2,1,0:T(8,128)}) %reduce-scatter.5.cloned.1.call-update) | async-done | bytes 2097168 | tf_op jit(solution)/shard_map/reduce_scatter | solution.py:45
  826.6 6.5 convolution_bitcast_fusion
  833.1 125.8 %all-reduce.3.cloned.1.call-done = f32[256,256]{0,1:T(8,128)} async-done(((f32[256,256]{0,1:T(8,128)}), f32[256,256]{0,1:T(8,128)}) %all-reduce.3.cloned.1.call-update) | async-done | bytes 262160 | tf_op jit(solution)/shard_map/psum | solution.py:50
  961.0 11.7 %cholesky.50 = f32[128,128]{1,0:T(8,128)S(1)} custom-call(f32[128,128]{1,0:T(8,128)S(1)} %cholesky.118), custom_call_target="Cholesky" | custom-call | tf_op jit(solution)/shard_map/jit(cholesky)/cholesky | solution.py:51
  972.8 9.8 custom-call.15
  983.1 11.9 %cholesky.105 = f32[128,128]{1,0:T(8,128)S(1)} custom-call(f32[128,128]{1,0:T(8,128)S(1)} %convolution_subtract_fusion.1), custom_call_target="Cholesky" | custom-call | tf_op jit(solution)/shard_map/jit(cholesky)/cholesky | solution.py:51
  1001.1 19.7 %custom-call.16 = f32[2,128,128]{1,2,0:T(8,128)S(1)} custom-call(f32[2,128,128]{2,1,0:T(8,128)S(1)} %get-tuple-element.65), custom_call_target="InvertDiagBlocksLowerTriangular" | custom-call | tf_op jit(solution)/shard_map/jit(_solve_triangular)/triangular_solve | solution.py:52
  (111 shorter events, 147.0 us)
Async XLA Ops:
  7.2 130.5 %all-gather.3.cloned.1.call-start = ((), (), s32[]{:S(2)}) async-start(), calls=%async_computation.2 | async-start | bytes 9437184 | tf_op jit(solution)/shard_map/all_gather | solution.py:20
  7.9 286.4 %reduce-scatter.3.cloned.1.call-start = ((), (), s32[]{:S(2)}) async-start(), calls=%async_computation.3 | async-start | bytes 10485760 | tf_op jit(solution)/shard_map/reduce_scatter | solution.py:30
  224.6 107.0 %all-gather.5.cloned.1.call-start = ((), (), s32[]{:S(2)}) async-start(), calls=%async_computation.4 | async-start | bytes 5242880 | tf_op jit(solution)/shard_map/all_gather | solution.py:33
  297.0 529.6 %reduce-scatter.5.cloned.1.call-start = ((), (), s32[]{:S(2)}) async-start(), calls=%async_computation.5 | async-start | bytes 18874368 | tf_op jit(solution)/shard_map/reduce_scatter | solution.py:45
  546.0 413.0 %all-reduce.3.cloned.1.call-start = ((), (), s32[]{:S(2)}) async-start(), calls=%async_computation.6 | async-start | bytes 524288 | tf_op jit(solution)/shard_map/psum | solution.py:50
  826.6 194.3 %copy-start = (f32[128,16,256]{2,1,0:T(8,128)S(1)}, f32[128,16,256]{2,1,0:T(8,128)}, u32[]{:S(2)}) copy-start(f32[128,16,256]{2,1,0:T(8,128)} %reduce-scatter.5.cloned.1.call-done) | copy-start | bytes 6291460
Sparse Core Ops, SparseCore 0:
  10.0 127.6 all-gather.2
  224.8 69.4 reduce-scatter.2
  297.1 34.4 all-gather.4
  546.1 280.3 reduce-scatter.4
  833.2 125.6 all-reduce.2
where the time goes:
time: 1040 us; the launch traced here: 1030 us
  waiting for transfers between devices  619 us (60%)
  other arithmetic  215 us (21%)
  matrix products  97 us (9%)
  local copies, waits for them, and re-layouts  88 us (8%)
  between operations  15.2 us (1%)
    reduce_scatter x1, waiting for transfers between devices, local(): range_rows = lax.psum_scatter(total, 'pix', scatter_dimension=1, tiled=True)  280 us
    scatter-add x8, other arithmetic, step(): total.at[tile_ids.reshape(-1)].add(contrib.reshape(-1, block_size, width))  157 us
    all_gather x1, waiting for transfers between devices, local(): full_sketch = lax.all_gather(sketch, 'pix', axis=1, tiled=True)  129 us
    psum x1, waiting for transfers between devices, local(): gram = lax.psum(local_gram, ('pix', 'beam'))  126 us
    reduce_scatter x1, waiting for transfers between devices, local(): lax.psum_scatter(partial_sketch, 'beam', scatter_dimension=1, tiled=True)  69.6 us
    gather x8, local copies, waits for them, and re-layouts, pixel_pass(): picked = full_sketch[tile_ids]  49 us
    dot_general x8, matrix products, step(): jnp.einsum('tsab,tak->tsbk', tile_gains, tile_rows, preferred_element_typ...  48.9 us
    dot_general x8, matrix products, pixel_pass(): jnp.einsum('tsab,tsbk->tak', tile_gains, picked, preferred_element_type=j...  37.1 us
  transfers between devices with their start and end apart: 5, of which 5 were waited for; matrix products, arithmetic and copies ran while one was open for 2% of the time, Pallas kernels for 0%

commit v1 on v0

--- a/solution.py
+++ b/solution.py
@@ -47,7 +47,7 @@
     local_gram = jnp.dot(
         flat.T, flat, precision=lax.Precision.HIGHEST, preferred_element_type=jnp.float32
     )
-    gram = lax.psum(local_gram, ("pix", "beam"))
+    gram = jnp.sum(jax.lax.all_gather(local_gram, axis_name=("pix", "beam")), 0)
     lower = jnp.linalg.cholesky(gram)
     solved = jax.scipy.linalg.solve_triangular(lower, flat.T, lower=True).T
     scale = jnp.sqrt(jnp.float32(BEAMS))

time: 1040 us -> 988 us (0.950)
  waiting for transfers between devices: 619 us -> 567 us
    psum x1 -> x0, waiting for transfers between devices: 126 us -> none  [local(): gram = lax.psum(local_gram, ('pix', 'beam'))]
    all_gather x0 -> x1, waiting for transfers between devices: none -> 74.2 us  [local(): gram = jnp.sum(jax.lax.all_gather(local_gram, axis_name=('pix', 'beam')), 0)]
    unnamed x5 -> x3, local copies, waits for them, and re-layouts: 22.9 us -> 22.9 us
where the time goes in v1:
time: 988 us; the launch traced here: 986 us
  waiting for transfers between devices  567 us (57%)
  other arithmetic  218 us (22%)
  matrix products  96.1 us (10%)
  local copies, waits for them, and re-layouts  89.2 us (9%)
  between operations  15.2 us (2%)
    reduce_scatter x1, waiting for transfers between devices, local(): range_rows = lax.psum_scatter(total, 'pix', scatter_dimension=1, tiled=True)  281 us
    scatter-add x8, other arithmetic, step(): total.at[tile_ids.reshape(-1)].add(contrib.reshape(-1, block_size, width))  157 us
    all_gather x1, waiting for transfers between devices, local(): full_sketch = lax.all_gather(sketch, 'pix', axis=1, tiled=True)  129 us
    all_gather x1, waiting for transfers between devices, local(): gram = jnp.sum(jax.lax.all_gather(local_gram, axis_name=('pix', 'beam')), 0)  74.2 us
    reduce_scatter x1, waiting for transfers between devices, local(): lax.psum_scatter(partial_sketch, 'beam', scatter_dimension=1, tiled=True)  69.5 us
    gather x8, local copies, waits for them, and re-layouts, pixel_pass(): picked = full_sketch[tile_ids]  49.1 us
    dot_general x8, matrix products, step(): jnp.einsum('tsab,tak->tsbk', tile_gains, tile_rows, preferred_element_typ...  48.9 us
    dot_general x8, matrix products, pixel_pass(): jnp.einsum('tsab,tsbk->tak', tile_gains, picked, preferred_element_type=j...  37.1 us
  transfers between devices with their start and end apart: 5, of which 5 were waited for; matrix products, arithmetic and copies ran while one was open for 2% of the time, Pallas kernels for 0%

profile of v1, /device:TPU:0, one launch (start us, length us, event | category | flops | bytes accessed | tf_op | source)
XLA Modules:
  0.0 986.4 jit_solution(82709423209850582)
XLA Ops:
  8.7 129.0 %all-gather.5.cloned.1.call-done = bf16[128,128,256]{2,1,0:T(8,128)(2,1)} async-done(((bf16[128,16,256]{2,1,0:T(8,128)(2,1)}), bf16[128,128,256]{2,1,0:T(8,128)(2,1)}) %all-gather.5.cloned.1.call-update) | async-done | bytes 8388624 | tf_op jit(solution)/shard_map/all_gather | solution.py:20
  137.7 87.0 %while.21 = (s32[]{:T(128)}, f32[8,8,128,256]{3,2,1,0:T(8,128)}, bf16[8,8,8,128,128]{4,3,2,1,0:T(8,128)(2,1)}, s32[8,8,8]{2,1,0:T(8,128)S(1)}, bf16[128,128,256]{2,1,0:T(8,128)(2,1)}, /*index=5*/s32[]{:T(128)}) while((s32[]{:T(128)}, f32[8,8,128,256]{3,2,1,0:T(8,128)}, bf16[8,8,8,128,128]{4,3,2,1,0:T(8,128)(2,1)}, s32[8,8,8]{2,1,0:T(8,128)S(1)}, ...), condition=%wide.region_1.2_spmd, body=%wide.region_0.1_spmd.sunk | while | flops 536872128 | bytes 15735369 | solution.py:27
  137.8 6.1 gather_fusion
  148.7 6.1 gather_fusion
  224.8 69.5 %reduce-scatter.3.cloned.1.call-done = f32[64,32,256]{2,1,0:T(8,128)} async-done(((f32[64,128,256]{2,1,0:T(8,128)}), f32[64,32,256]{2,1,0:T(8,128)}) %reduce-scatter.3.cloned.1.call-update) | async-done | bytes 2097168 | tf_op jit(solution)/shard_map/reduce_scatter | solution.py:30
  297.1 21.3 %copy.29 = bf16[64,8,128,128]{2,3,1,0:T(8,128)(2,1)} copy(bf16[64,8,128,128]{3,2,1,0:T(8,128)(2,1)} %bitcast.101) | data formatting | bytes 33554432 | tf_op args[1]
  318.4 13.3 %all-gather.7.cloned.1.call-done = bf16[64,128,256]{2,1,0:T(8,128)(2,1)} async-done(((bf16[64,32,256]{2,1,0:T(8,128)(2,1)}), bf16[64,128,256]{2,1,0:T(8,128)(2,1)}) %all-gather.7.cloned.1.call-update) | async-done | bytes 4194320 | tf_op jit(solution)/shard_map/all_gather | solution.py:33
  331.7 7.8 broadcast_in_dim.14
  339.5 206.9 %while.22 = (s32[]{:T(128)}, f32[128,128,256]{2,1,0:T(8,128)}, s32[8,8,8]{2,1,0:T(8,128)S(1)}, bf16[8,8,8,128,128]{3,4,2,1,0:T(8,128)(2,1)}, bf16[8,8,128,256]{3,2,1,0:T(8,128)(2,1)}, /*index=5*/s32[]{:T(128)}) while((s32[]{:T(128)}, f32[128,128,256]{2,1,0:T(8,128)}, s32[8,8,8]{2,1,0:T(8,128)S(1)}, bf16[8,8,8,128,128]{3,4,2,1,0:T(8,128)(2,1)}, ...), condition=%wide.region_5.6_spmd, body=%wide.region_3.5_spmd.sunk | while | flops 538968256 | bytes 36178760 | solution.py:44
  345.7 19.6 %scatter_fusion = f32[128,128,256]{2,1,0:T(8,128)} fusion(f32[128,128,256]{2,1,0:T(8,128)} %get-tuple-element.250, s32[64]{0:T(128)S(1)} %fusion.48, f32[64,128,256]{2,1,0:T(8,128)} %bitcast.97), kind=kCustom, calls=%fused_computation.1.clone.1 | custom fusion | flops 2097152 | bytes 25166080 | tf_op jit(solution)/shard_map/while/body/eval_jaxpr/scatter-add | solution.py:41
  371.5 19.8 %scatter_fusion = f32[128,128,256]{2,1,0:T(8,128)} fusion(f32[128,128,256]{2,1,0:T(8,128)} %get-tuple-element.250, s32[64]{0:T(128)S(1)} %fusion.48, f32[64,128,256]{2,1,0:T(8,128)} %bitcast.97), kind=kCustom, calls=%fused_computation.1.clone.1 | custom fusion | flops 2097152 | bytes 25166080 | tf_op jit(solution)/shard_map/while/body/eval_jaxpr/scatter-add | solution.py:41
  397.4 19.8 %scatter_fusion = f32[128,128,256]{2,1,0:T(8,128)} fusion(f32[128,128,256]{2,1,0:T(8,128)} %get-tuple-element.250, s32[64]{0:T(128)S(1)} %fusion.48, f32[64,128,256]{2,1,0:T(8,128)} %bitcast.97), kind=kCustom, calls=%fused_computation.1.clone.1 | custom fusion | flops 2097152 | bytes 25166080 | tf_op jit(solution)/shard_map/while/body/eval_jaxpr/scatter-add | solution.py:41
  423.5 19.6 %scatter_fusion = f32[128,128,256]{2,1,0:T(8,128)} fusion(f32[128,128,256]{2,1,0:T(8,128)} %get-tuple-element.250, s32[64]{0:T(128)S(1)} %fusion.48, f32[64,128,256]{2,1,0:T(8,128)} %bitcast.97), kind=kCustom, calls=%fused_computation.1.clone.1 | custom fusion | flops 2097152 | bytes 25166080 | tf_op jit(solution)/shard_map/while/body/eval_jaxpr/scatter-add | solution.py:41
  449.3 19.8 %scatter_fusion = f32[128,128,256]{2,1,0:T(8,128)} fusion(f32[128,128,256]{2,1,0:T(8,128)} %get-tuple-element.250, s32[64]{0:T(128)S(1)} %fusion.48, f32[64,128,256]{2,1,0:T(8,128)} %bitcast.97), kind=kCustom, calls=%fused_computation.1.clone.1 | custom fusion | flops 2097152 | bytes 25166080 | tf_op jit(solution)/shard_map/while/body/eval_jaxpr/scatter-add | solution.py:41
  475.2 19.5 %scatter_fusion = f32[128,128,256]{2,1,0:T(8,128)} fusion(f32[128,128,256]{2,1,0:T(8,128)} %get-tuple-element.250, s32[64]{0:T(128)S(1)} %fusion.48, f32[64,128,256]{2,1,0:T(8,128)} %bitcast.97), kind=kCustom, calls=%fused_computation.1.clone.1 | custom fusion | flops 2097152 | bytes 25166080 | tf_op jit(solution)/shard_map/while/body/eval_jaxpr/scatter-add | solution.py:41
  500.9 19.6 %scatter_fusion = f32[128,128,256]{2,1,0:T(8,128)} fusion(f32[128,128,256]{2,1,0:T(8,128)} %get-tuple-element.250, s32[64]{0:T(128)S(1)} %fusion.48, f32[64,128,256]{2,1,0:T(8,128)} %bitcast.97), kind=kCustom, calls=%fused_computation.1.clone.1 | custom fusion | flops 2097152 | bytes 25166080 | tf_op jit(solution)/shard_map/while/body/eval_jaxpr/scatter-add | solution.py:41
  526.8 19.7 %scatter_fusion = f32[128,128,256]{2,1,0:T(8,128)} fusion(f32[128,128,256]{2,1,0:T(8,128)} %get-tuple-element.250, s32[64]{0:T(128)S(1)} %fusion.48, f32[64,128,256]{2,1,0:T(8,128)} %bitcast.97), kind=kCustom, calls=%fused_computation.1.clone.1 | custom fusion | flops 2097152 | bytes 25166080 | tf_op jit(solution)/shard_map/while/body/eval_jaxpr/scatter-add | solution.py:41
  546.5 280.7 %reduce-scatter.5.cloned.1.call-done = f32[128,16,256]{2,1,0:T(8,128)} async-done(((f32[128,128,256]{2,1,0:T(8,128)}), f32[128,16,256]{2,1,0:T(8,128)}) %reduce-scatter.5.cloned.1.call-update) | async-done | bytes 2097168 | tf_op jit(solution)/shard_map/reduce_scatter | solution.py:45
  827.2 6.4 convolution_bitcast_fusion
  835.8 74.2 %all-gather.9.cloned.1.call-done = f32[8192,256]{1,0:T(8,128)} async-done(((f32[256,256]{1,0:T(8,128)}), f32[8192,256]{1,0:T(8,128)}) %all-gather.9.cloned.1.call-update) | async-done | bytes 8388624 | tf_op jit(solution)/shard_map/all_gather | solution.py:50
  914.1 11.7 %cholesky.50 = f32[128,128]{1,0:T(8,128)S(1)} custom-call(f32[128,128]{1,0:T(8,128)S(1)} %cholesky.118), custom_call_target="Cholesky" | custom-call | tf_op jit(solution)/shard_map/jit(cholesky)/cholesky | solution.py:51
  925.9 9.8 custom-call.15
  936.2 11.7 %cholesky.105 = f32[128,128]{1,0:T(8,128)S(1)} custom-call(f32[128,128]{1,0:T(8,128)S(1)} %convolution_subtract_fusion.1), custom_call_target="Cholesky" | custom-call | tf_op jit(solution)/shard_map/jit(cholesky)/cholesky | solution.py:51
  954.0 19.9 %custom-call.16 = f32[2,128,128]{1,2,0:T(8,128)S(1)} custom-call(f32[2,128,128]{2,1,0:T(8,128)S(1)} %get-tuple-element.65), custom_call_target="InvertDiagBlocksLowerTriangular" | custom-call | tf_op jit(solution)/shard_map/jit(_solve_triangular)/triangular_solve | solution.py:52
  (111 shorter events, 150.2 us)
Async XLA Ops:
  7.2 130.5 %all-gather.5.cloned.1.call-start = ((), (), s32[]{:S(2)}) async-start(), calls=%async_computation.2 | async-start | bytes 9437184 | tf_op jit(solution)/shard_map/all_gather | solution.py:20
  7.9 286.4 %reduce-scatter.3.cloned.1.call-start = ((), (), s32[]{:S(2)}) async-start(), calls=%async_computation.3 | async-start | bytes 10485760 | tf_op jit(solution)/shard_map/reduce_scatter | solution.py:30
  224.7 107.0 %all-gather.7.cloned.1.call-start = ((), (), s32[]{:S(2)}) async-start(), calls=%async_computation.4 | async-start | bytes 5242880 | tf_op jit(solution)/shard_map/all_gather | solution.py:33
  297.1 530.1 %reduce-scatter.5.cloned.1.call-start = ((), (), s32[]{:S(2)}) async-start(), calls=%async_computation.5 | async-start | bytes 18874368 | tf_op jit(solution)/shard_map/reduce_scatter | solution.py:45
  546.4 363.5 %all-gather.9.cloned.1.call-start = ((), (), s32[]{:S(2)}) async-start(), calls=%async_computation.6 | async-start | bytes 8650752 | tf_op jit(solution)/shard_map/all_gather | solution.py:50
Sparse Core Ops, SparseCore 0:
  10.0 127.6 all-gather.4
  224.8 69.4 reduce-scatter.2
  297.2 34.4 all-gather.6
  546.6 280.5 reduce-scatter.4
  833.8 76.1 all-gather.8
